TPU v7x, 128 devices: a whole 4x4x4 slice. The times are simulated.
128 devices in a mesh: dp: 8 (over x_lo, y), expert: 16 (over x_hi, z, core).
Axes of the slice: x: 4 (x_hi: 2, x_lo: 2; x = x_hi * 2 + x_lo), y: 4, z: 4, core: 2. Of those that a mesh axis runs over, the one named last changes fastest.
Arguments:
- tokens: bfloat16 [65536, 2048], P(('dp', 'expert')), may hold values from -6 to 6
- probe: bfloat16 [65536, 2048], P(('dp', 'expert')), may hold values from -20 to 20
- domain: int32 [65536], P(('dp', 'expert')), may hold values from 0 to 21
- mix: float32 [22], replicated, may hold values from 0.5 to 2
- router: bfloat16 [2048, 32], replicated, may hold values from -0.125 to 0.125
- picks: int32 [128, 32, 40], P(('dp', 'expert')), may hold values from 0 to 511, as said below
- w_gate: bfloat16 [2048, 32, 768], P(None, 'expert'), may hold values from -0.125 to 0.125
- w_up: bfloat16 [2048, 32, 768], P(None, 'expert'), may hold values from -0.125 to 0.125
- w_down: bfloat16 [2048, 32, 768], P(None, 'expert'), may hold values from -0.21875 to 0.21875
Outputs:
- domain_loss: float32 [22], replicated
- router_grad: float32 [2048, 32], replicated
- grad_gate: bfloat16 [2048, 32, 768], P('dp', 'expert')
- grad_up: bfloat16 [2048, 32, 768], P('dp', 'expert')
- grad_down: bfloat16 [2048, 32, 768], P('dp', 'expert')
Inputs may be any that keep to these rules, and one draw needn't show every extreme that they name: The 40 picks of one expert on one device are distinct token positions of that device.
All inputs are finite; a program needn't handle non-finite values.
Results may differ from a plain program's by a relative error of at most 0.018.
Values may be sent and summed in bfloat16 or wider, within the bound.
A program may use at most 192 MiB of HBM per device.

v0:
```python
import math
import jax
import jax.numpy as jnp
from jax import lax
from jax.sharding import PartitionSpec as P

BF = jnp.bfloat16
F32 = jnp.float32


def body(tokens, probe, domain, mix, router, picks, w_gate, w_up, w_down):
    token_count, model_width = tokens.shape
    expert_count = router.shape[1]
    slot_count = picks.shape[2]
    pick_count = expert_count * slot_count
    domain_count = mix.shape[0]
    device_count = lax.axis_size("dp") * lax.axis_size("expert")
    flat = picks[0].reshape(pick_count)
    token_ids = jnp.arange(token_count, dtype=jnp.int32)
    select = (flat[:, None] == token_ids[None, :]).astype(BF)
    expert_of = jnp.repeat(jnp.arange(expert_count, dtype=jnp.int32), slot_count)
    own_expert = expert_of[:, None] == jnp.arange(expert_count, dtype=jnp.int32)[None, :]
    outgoing = jnp.dot(select, tokens, preferred_element_type=F32).astype(BF)
    received = lax.all_to_all(
        outgoing.reshape(expert_count, 1, slot_count, model_width),
        "expert",
        split_axis=0,
        concat_axis=1,
        tiled=True,
    )
    logits = jnp.dot(outgoing, router, preferred_element_type=F32)
    gate = jax.nn.sigmoid(jnp.sum(jnp.where(own_expert, logits, 0.0), axis=1))
    pre_gate = jnp.einsum("jsrd,djf->jsrf", received, w_gate, preferred_element_type=F32)
    pre_up = jnp.einsum("jsrd,djf->jsrf", received, w_up, preferred_element_type=F32)
    hidden = (jax.nn.silu(pre_gate) * pre_up).astype(BF)
    result = jnp.einsum("jsrf,djf->jsrd", hidden, w_down, preferred_element_type=F32).astype(BF)
    returned = lax.all_to_all(result, "expert", split_axis=1, concat_axis=0, tiled=True)
    returned = returned.reshape(pick_count, model_width)
    weighted = jnp.where(
        flat[None, :] == token_ids[:, None], gate.astype(BF)[None, :], jnp.zeros((), BF)
    )
    added = jnp.dot(weighted, returned, preferred_element_type=F32)
    difference = tokens.astype(F32) + added - probe.astype(F32)
    per_token = jnp.sum(difference * difference, axis=1)
    member = (domain[:, None] == jnp.arange(domain_count, dtype=jnp.int32)[None, :]).astype(F32)
    local_loss = jnp.sum(per_token[:, None] * member, axis=0)
    loss_scale = 1.0 / math.sqrt(device_count * slot_count)
    weight_tok = jnp.sum(member * mix[None, :], axis=1)
    upstream = ((loss_scale * weight_tok)[:, None] * difference).astype(BF)
    picked_up = jnp.dot(select, upstream, preferred_element_type=F32)
    sending = (gate[:, None] * picked_up).astype(BF)
    gate_slope = jnp.sum(picked_up * returned.astype(F32), axis=1)
    logit_grad = gate_slope * gate * (1.0 - gate)
    placing = jnp.where(own_expert, logit_grad[:, None], 0.0)
    high = placing.astype(BF)
    low = (placing - high.astype(F32)).astype(BF)
    placed = lax.dot_general(
        select,
        jnp.concatenate([high, low], axis=1),
        (((0,), (0,)), ((), ())),
        preferred_element_type=F32,
    ).astype(BF)
    router_part = lax.dot_general(
        tokens, placed, (((0,), (0,)), ((), ())), preferred_element_type=F32
    )
    router_part = router_part[:, :expert_count] + router_part[:, expert_count:]
    loss_rows = jnp.zeros((8, expert_count), F32).at[0, :domain_count].set(local_loss)
    summed = lax.psum(jnp.concatenate([router_part, loss_rows], axis=0), ("dp", "expert"))
    back_grad = lax.all_to_all(
        sending.reshape(expert_count, 1, slot_count, model_width),
        "expert",
        split_axis=0,
        concat_axis=1,
        tiled=True,
    )

    def reduced(left, right):
        part = jnp.einsum("jsrd,jsrf->djf", left, right, preferred_element_type=F32)
        return lax.psum_scatter(part.astype(BF), "dp", scatter_dimension=0, tiled=True)

    grad_down = reduced(back_grad, hidden)
    hidden_grad = jnp.einsum("jsrd,djf->jsrf", back_grad, w_down, preferred_element_type=F32)
    sigmoid_gate = jax.nn.sigmoid(pre_gate)
    gate_in = (
        hidden_grad * pre_up * sigmoid_gate * (1.0 + pre_gate * (1.0 - sigmoid_gate))
    ).astype(BF)
    up_in = (hidden_grad * (pre_gate * sigmoid_gate)).astype(BF)
    grad_gate = reduced(received, gate_in)
    grad_up = reduced(received, up_in)
    domain_loss = summed[model_width, :domain_count] * (
        domain_count / (token_count * device_count * model_width)
    )
    return (domain_loss, summed[:model_width], grad_gate, grad_up, grad_down)


def solution(mesh):
    placed = (
        P(("dp", "expert"), None),
        P(("dp", "expert"), None),
        P(("dp", "expert")),
        P(),
        P(),
        P(("dp", "expert"), None, None),
        P(None, "expert", None),
        P(None, "expert", None),
        P(None, "expert", None),
    )
    return jax.shard_map(
        body,
        mesh=mesh,
        in_specs=placed,
        out_specs=(
            P(),
            P(),
            P("dp", "expert", None),
            P("dp", "expert", None),
            P("dp", "expert", None),
        ),
        check_vma=False,
    )
```

profile of v0, /device:TPU:1, one launch (start us, length us, event | category | flops | bytes accessed | tf_op | source)
XLA Modules:
  0.0 530.8 jit_solution(12913081817586084446)
XLA Ops:
  8.0 0.0 copy-start
  8.0 0.8 eq.64
  8.9 4.9 convolution_convert_fusion
  13.8 0.0 copy-start.7
  13.8 0.0 slice-start
  13.8 71.2 %all_to_all.51 = bf16[32,1,40,2048]{3,2,1,0:T(8,128)(2,1)S(1)} all-to-all(bf16[32,1,40,2048]{3,2,1,0:T(8,128)(2,1)S(1)} %bitcast.69), channel_id=1, replica_groups=mesh['dp'=8,'expert'=16] {'expert'}, dimensions={0} | all-to-all | bytes 10485760 | tf_op jit(solution)/shard_map/all_to_all | solution.py:24
  85.0 4.4 fusion.5
  89.4 0.0 copy-start.8
  89.4 0.0 copy-done.3
  89.4 0.0 slice-done
  89.4 0.0 slice-done.1
  89.4 6.5 %multiply_convert_fusion.4 = (bf16[2,16,40,768]{3,2,1,0:T(8,128)(2,1)}, f32[2,16,40,768]{3,2,1,0:T(8,128)}) fusion(f32[2,16,40,768]{3,2,1,0:T(8,128)S(1)} %fusion.5, bf16[2048,2,768,1]{2,1,0,3:T(2,128)(2,1)S(1)} %bitcast.79, bf16[16,2,1,40,2048]{4,3,1,0,2:T(8,128)(2,1)S(1)} %bitcast.71), kind=kOutput, calls=%fused_computation.31 | convolution fusion | flops 4032430080 | bytes 21364736 | tf_op jit(solution)/shard_map/jsrd,djf->jsrf/dot_general | solution.py:34
  96.0 7.7 %fusion.19 = bf16[2,16,40,2048]{3,2,1,0:T(8,128)(2,1)S(1)} fusion(bf16[2,16,40,768]{3,2,1,0:T(8,128)(2,1)} %get-tuple-element.43, bf16[2048,2,768,1]{2,1,0,3:T(2,128)(2,1)} %bitcast.80), kind=kOutput, calls=%fused_computation.28 | convolution fusion | flops 4029153280 | bytes 13500416 | tf_op jit(solution)/shard_map/jsrf,djf->jsrd/dot_general | solution.py:36
  103.6 2.8 copy.51
  106.4 5.7 %all-to-all-start.1 = ((bf16[2,16,40,2048]{3,2,0,1:T(8,128)(2,1)}), bf16[2,16,40,2048]{3,2,0,1:T(8,128)(2,1)}, u32[]{:S(2)}, u32[]{:S(2)}) async-start(bf16[2,16,40,2048]{3,2,0,1:T(8,128)(2,1)} %copy.51), calls=%async_computation.1 | async-start | bytes 10485760 | tf_op jit(solution)/shard_map/all_to_all | solution.py:37
  112.2 0.1 eq.68
  112.2 4.3 fusion.38
  116.6 64.9 %all-to-all-done.1 = bf16[2,16,40,2048]{3,2,0,1:T(8,128)(2,1)} async-done(((bf16[2,16,40,2048]{3,2,0,1:T(8,128)(2,1)}), bf16[2,16,40,2048]{3,2,0,1:T(8,128)(2,1)}, u32[]{:S(2)}, u32[]{:S(2)}) %all-to-all-start.1) | async-done | bytes 5242912 | tf_op jit(solution)/shard_map/all_to_all | solution.py:37
  181.5 6.5 %multiply_reduce_fusion.1 = (f32[512]{0:T(512)S(1)}, f32[512,2048]{1,0:T(8,128)S(1)}) fusion(bf16[512,2048]{1,0:T(8,128)(2,1)} %param.12, bf16[1280,2048]{1,0:T(8,128)(2,1)} %bitcast.11, s32[1280]{0:T(1024)S(1)} %eq.64, bf16[1280]{0:T(1024)(128)(2,1)S(1)} %get-tuple-element.42, bf16[512,2048]{1,0:T(8,128)(2,1)S(1)} %copy-done.4), kind=kOutput, calls=%fused_computation.25 | convolution fusion | flops 2691956224 | bytes 13641216 | tf_op jit(solution)/shard_map/dot_general | solution.py:42
  188.0 0.1 select_reduce_fusion.1
  188.1 7.4 %multiply_convert_fusion = (bf16[1280,2048]{1,0:T(8,128)(2,1)}, f32[1280]{0:T(1024)S(1)}) fusion(f32[1280]{0:T(1024)S(1)} %get-tuple-element.41, bf16[2,16,40,2048]{3,2,0,1:T(8,128)(2,1)} %all-to-all-done.1, f32[512,2048]{1,0:T(8,128)S(1)} %get-tuple-element.46, f32[512]{0:T(512)S(1)} %broadcast_multiply_fusion, s32[1280]{0:T(1024)S(1)} %eq.64), kind=kOutput, calls=%fused_computation.3 | convolution fusion | flops 2700212992 | bytes 14697472 | tf_op jit(solution)/shard_map/dot_general | solution.py:50
  195.5 14.7 %all-to-all-start.2 = ((bf16[32,1,40,2048]{3,2,1,0:T(8,128)(2,1)}), bf16[32,1,40,2048]{3,2,1,0:T(8,128)(2,1)}, u32[]{:S(2)}, u32[]{:S(2)}) async-start(bf16[32,1,40,2048]{3,2,1,0:T(8,128)(2,1)} %bitcast.74), calls=%async_computation.2 | async-start | bytes 10485760 | tf_op jit(solution)/shard_map/all_to_all | solution.py:69
  210.2 0.0 all-reduce.3.cloned.1.call-start
  210.2 0.1 copy.52
  210.4 1.0 convolution_bitcast_fusion
  211.5 0.7 select_maximum_fusion
  212.2 0.0 all-reduce.3.cloned.1.call-update
  212.2 0.0 reduce-scatter.8.cloned.1.call-start
  212.3 68.4 %all-to-all-done.2 = bf16[32,1,40,2048]{3,2,1,0:T(8,128)(2,1)} async-done(((bf16[32,1,40,2048]{3,2,1,0:T(8,128)(2,1)}), bf16[32,1,40,2048]{3,2,1,0:T(8,128)(2,1)}, u32[]{:S(2)}, u32[]{:S(2)}) %all-to-all-start.2) | async-done | bytes 5242912 | tf_op jit(solution)/shard_map/all_to_all | solution.py:69
  280.7 9.8 %fusion.2 = bf16[2048,2,768]{0,2,1:T(8,128)(2,1)} fusion(bf16[2,16,40,768]{3,2,1,0:T(8,128)(2,1)} %get-tuple-element.43, bf16[16,2,1,40,2048]{4,3,1,0,2:T(8,128)(2,1)} %bitcast.18), kind=kOutput, calls=%fused_computation.8 | convolution fusion | flops 4029677568 | bytes 13500416 | tf_op jit(solution)/shard_map/jsrd,jsrf->djf/dot_general | solution.py:78
  290.5 0.0 reduce-scatter.8.cloned.1.call-update
  290.5 0.3 reduce-scatter.6.cloned.1.call-start
  290.8 8.2 %fusion.7 = f32[2,16,40,768]{3,2,1,0:T(8,128)S(1)} fusion(bf16[2048,2,768,1]{2,1,0,3:T(2,128)(2,1)} %bitcast.81, bf16[16,2,1,40,2048]{4,3,1,0,2:T(8,128)(2,1)} %bitcast.18), kind=kOutput, calls=%fused_computation.13 | convolution fusion | flops 4026531840 | bytes 15466496 | tf_op jit(solution)/shard_map/jsrd,djf->jsrf/dot_general | solution.py:82
  299.0 1.8 copy-done.10
  300.9 9.9 %fusion.1 = bf16[2048,2,768]{0,2,1:T(8,128)(2,1)} fusion(bf16[16,2,1,40,2048]{4,3,1,0,2:T(8,128)(2,1)} %bitcast.72, f32[2,16,40,768]{3,2,1,0:T(8,128)S(1)} %fusion.7, f32[2,16,40,768]{3,2,1,0:T(8,128)S(1)} %copy-done.9), kind=kOutput, calls=%fused_computation.7 | convolution fusion | flops 4035575808 | bytes 19398656 | tf_op jit(solution)/shard_map/jsrd,jsrf->djf/dot_general | solution.py:78
  310.8 0.0 reduce-scatter.6.cloned.1.call-update
  310.8 0.0 reduce-scatter.4.cloned.1.call-start
  310.8 12.3 %fusion = bf16[2048,2,768]{0,2,1:T(8,128)(2,1)} fusion(bf16[16,2,1,40,2048]{4,3,1,0,2:T(8,128)(2,1)} %bitcast.73, f32[2,16,40,768]{3,2,1,0:T(8,128)} %copy-done.8, f32[2,16,40,768]{3,2,1,0:T(8,128)} %copy-done.10, f32[2,16,40,768]{3,2,1,0:T(8,128)} %get-tuple-element.44), kind=kOutput, calls=%fused_computation.6 | convolution fusion | flops 4039507968 | bytes 23330816 | tf_op jit(solution)/shard_map/jsrd,jsrf->djf/dot_general | solution.py:78
  323.1 0.0 reduce-scatter.4.cloned.1.call-update
  323.1 0.0 copy-start.1
  323.2 129.6 %all-reduce.3.cloned.1.call-done = f32[2056,32]{0,1:T(8,128)} async-done(((f32[2056,32]{0,1:T(8,128)}), f32[2056,32]{0,1:T(8,128)}) %all-reduce.3.cloned.1.call-update) | async-done | bytes 263184 | tf_op jit(solution)/shard_map/psum | solution.py:68
  452.8 1.7 slice.35
  454.4 1.3 fusion.49
  455.8 3.1 copy.58
  458.9 3.0 copy.57
  461.9 58.3 %reduce-scatter.4.cloned.1.call-done = bf16[256,2,768]{0,2,1:T(8,128)(2,1)} async-done(((bf16[2048,2,768]{0,2,1:T(8,128)(2,1)}), bf16[256,2,768]{0,2,1:T(8,128)(2,1)}) %reduce-scatter.4.cloned.1.call-update) | async-done | bytes 786448 | tf_op jit(solution)/shard_map/reduce_scatter | solution.py:79
  520.2 3.0 copy.56
  523.3 0.0 copy-done.1
  (26 shorter events, 0.1 us)
Async XLA Ops:
  8.0 104.2 %copy-start = (bf16[2048,32]{0,1:T(8,128)(2,1)S(1)}, bf16[2048,32]{0,1:T(8,128)(2,1)}, u32[]{:S(2)}) copy-start(bf16[2048,32]{0,1:T(8,128)(2,1)} %param.15) | copy-start | bytes 393220
  13.8 71.2 %copy-start.2 = (bf16[1280,2048]{1,0:T(8,128)(2,1)}, bf16[1280,2048]{1,0:T(8,128)(2,1)S(1)}, u32[]{:S(2)}) copy-start(bf16[1280,2048]{1,0:T(8,128)(2,1)S(1)} %convolution_convert_fusion) | copy-start | bytes 15728644
  13.8 71.2 %copy-start.7 = (bf16[2048,2,768]{2,1,0:T(2,128)(2,1)S(1)}, bf16[2048,2,768]{2,1,0:T(2,128)(2,1)}, u32[]{:S(2)}) copy-start(bf16[2048,2,768]{2,1,0:T(2,128)(2,1)} %param.17) | copy-start | bytes 18874372
  13.8 75.6 %slice-start = ((s8[6291456]{0:T(1024)(128)(4,1)}), s8[4194304]{0:T(1024)(128)(4,1)S(1)}, s32[]{:S(2)}) async-start(s8[6291456]{0:T(1024)(128)(4,1)} %bitcast.77), calls=%async_computation.10 | async-start | bytes 8388608
  85.0 4.4 copy-start.3
  85.0 4.4 slice-start.1
  89.4 6.6 %copy-start.8 = (f32[2,16,40,768]{3,2,1,0:T(8,128)}, f32[2,16,40,768]{3,2,1,0:T(8,128)S(1)}, u32[]{:S(2)}) copy-start(f32[2,16,40,768]{3,2,1,0:T(8,128)S(1)} %fusion.5) | copy-start | bytes 11796484
  106.4 75.0 %all-to-all-start.1 = ((bf16[2,16,40,2048]{3,2,0,1:T(8,128)(2,1)}), bf16[2,16,40,2048]{3,2,0,1:T(8,128)(2,1)}, u32[]{:S(2)}, u32[]{:S(2)}) async-start(bf16[2,16,40,2048]{3,2,0,1:T(8,128)(2,1)} %copy.51), calls=%async_computation.1 | async-start | bytes 10485760 | tf_op jit(solution)/shard_map/all_to_all | solution.py:37
  112.1 69.3 %copy-start.4 = (bf16[512,2048]{1,0:T(8,128)(2,1)S(1)}, bf16[512,2048]{1,0:T(8,128)(2,1)}, u32[]{:S(2)}) copy-start(bf16[512,2048]{1,0:T(8,128)(2,1)} %param.11) | copy-start | bytes 6291460
  181.5 6.5 %copy-start.5 = (s32[512]{0:T(512)S(1)}, s32[512]{0:T(512)}, u32[]{:S(2)}) copy-start(s32[512]{0:T(512)} %param.13) | copy-start | bytes 6148
  181.5 6.5 %copy-start.6 = (f32[22]{0:T(128)S(1)}, f32[22]{0:T(128)}, u32[]{:S(2)}) copy-start(f32[22]{0:T(128)} %param.14) | copy-start | bytes 268
  195.5 85.2 %all-to-all-start.2 = ((bf16[32,1,40,2048]{3,2,1,0:T(8,128)(2,1)}), bf16[32,1,40,2048]{3,2,1,0:T(8,128)(2,1)}, u32[]{:S(2)}, u32[]{:S(2)}) async-start(bf16[32,1,40,2048]{3,2,1,0:T(8,128)(2,1)} %bitcast.74), calls=%async_computation.2 | async-start | bytes 10485760 | tf_op jit(solution)/shard_map/all_to_all | solution.py:69
  210.2 242.6 %all-reduce.3.cloned.1.call-start = ((), (), s32[]{:S(2)}) async-start(), calls=%async_computation.6 | async-start | bytes 557056 | tf_op jit(solution)/shard_map/psum | solution.py:68
  212.2 243.5 %reduce-scatter.8.cloned.1.call-start = ((), (), s32[]{:S(2)}) async-start(), calls=%async_computation.9 | async-start | bytes 7077888 | tf_op jit(solution)/shard_map/reduce_scatter | solution.py:79
  290.5 168.3 %reduce-scatter.6.cloned.1.call-start = ((), (), s32[]{:S(2)}) async-start(), calls=%async_computation.8 | async-start | bytes 7077888 | tf_op jit(solution)/shard_map/reduce_scatter | solution.py:79
  290.8 10.1 %copy-start.9 = (f32[2,16,40,768]{3,2,1,0:T(8,128)S(1)}, f32[2,16,40,768]{3,2,1,0:T(8,128)}, u32[]{:S(2)}) copy-start(f32[2,16,40,768]{3,2,1,0:T(8,128)} %copy-done.8) | copy-start | bytes 11796484
  299.0 1.9 copy-start.10
  310.8 209.4 %reduce-scatter.4.cloned.1.call-start = ((), (), s32[]{:S(2)}) async-start(), calls=%async_computation.7 | async-start | bytes 7077888 | tf_op jit(solution)/shard_map/reduce_scatter | solution.py:79
  323.1 200.1 %copy-start.1 = (bf16[2048,32]{0,1:T(8,128)(2,1)S(1)}, bf16[2048,32]{0,1:T(8,128)(2,1)}, u32[]{:S(2)}) copy-start(bf16[2048,32]{0,1:T(8,128)(2,1)} %param.15) | copy-start | bytes 393220
Sparse Core Ops, SparseCore 0:
  216.3 236.3 all-reduce.2
Sparse Core Ops, SparseCore 1:
  290.6 81.2 reduce-scatter.7
  374.2 71.8 reduce-scatter.5
  448.3 71.9 reduce-scatter.3
where the time goes:
time: 531 us
  waiting for transfers between devices  321 us (60%)
  matrix products  82.8 us (16%)
  blocking collectives  71.2 us (13%)
  starting transfers between devices  20.8 us (4%)
  local copies, waits for them, and re-layouts  16.6 us (3%)
  between operations  15.9 us (3%)
    psum x1, waiting for transfers between devices, body(): lax.psum(jnp.concatenate([router_part, loss_rows], axis=0), ('dp', 'exper...  130 us
    all_to_all x1, blocking collectives, body(): lax.all_to_all(outgoing.reshape(expert_count, 1, slot_count, model_width)...  71.2 us
    all_to_all x1, waiting for transfers between devices, body(): lax.all_to_all(sending.reshape(expert_count, 1, slot_count, model_width),...  68.4 us
    all_to_all x1, waiting for transfers between devices, body(): lax.all_to_all(result, 'expert', split_axis=1, concat_axis=0, tiled=True)  64.9 us
    reduce_scatter x3, waiting for transfers between devices, reduced(): lax.psum_scatter(part.astype(BF), 'dp', scatter_dimension=0, tiled=True)  58.3 us
    dot_general x3, matrix products, reduced(): part = jnp.einsum('jsrd,jsrf->djf', left, right, preferred_element_type=F32)  32 us
    all_to_all x1, starting transfers between devices, body(): lax.all_to_all(sending.reshape(expert_count, 1, slot_count, model_width),...  14.7 us
    unnamed x29, local copies, waits for them, and re-layouts  11.1 us
  transfers between devices with their start and end apart: 6, of which 4 were waited for; matrix products, arithmetic and copies ran while one was open for 10% of the time, Pallas kernels for 0%

commit v1 on v0

--- a/solution.py
+++ b/solution.py
@@ -34,7 +34,12 @@
     pre_up = jnp.einsum("jsrd,djf->jsrf", received, w_up, preferred_element_type=F32)
     hidden = (jax.nn.silu(pre_gate) * pre_up).astype(BF)
     result = jnp.einsum("jsrf,djf->jsrd", hidden, w_down, preferred_element_type=F32).astype(BF)
-    returned = lax.all_to_all(result, "expert", split_axis=1, concat_axis=0, tiled=True)
+    returned = jnp.concatenate(
+        lax.all_to_all(
+            jnp.stack(jnp.split(result, lax.axis_size("expert"), axis=1)), "expert", 0, 0
+        ),
+        axis=0,
+    )
     returned = returned.reshape(pick_count, model_width)
     weighted = jnp.where(
         flat[None, :] == token_ids[:, None], gate.astype(BF)[None, :], jnp.zeros((), BF)

time: 531 us -> 541 us (1.019)
  local copies, waits for them, and re-layouts: 16.6 us -> 25.9 us
    unnamed x29 -> x44, local copies, waits for them, and re-layouts: 11.1 us -> 22.4 us
where the time goes in v1:
time: 541 us; the launch traced here: 540 us
  waiting for transfers between devices  321 us (59%)
  matrix products  82.8 us (15%)
  blocking collectives  71.2 us (13%)
  local copies, waits for them, and re-layouts  25.9 us (5%)
  starting transfers between devices  20.8 us (4%)
  between operations  15.9 us (3%)
    psum x1, waiting for transfers between devices, body(): lax.psum(jnp.concatenate([router_part, loss_rows], axis=0), ('dp', 'exper...  130 us
    all_to_all x1, blocking collectives, body(): lax.all_to_all(outgoing.reshape(expert_count, 1, slot_count, model_width)...  71.2 us
    all_to_all x1, waiting for transfers between devices, body(): lax.all_to_all(sending.reshape(expert_count, 1, slot_count, model_width),...  68.4 us
    all_to_all x1, waiting for transfers between devices, body(): lax.all_to_all(jnp.stack(jnp.split(result, lax.axis_size('expert'), axis=...  64.9 us
    reduce_scatter x3, waiting for transfers between devices, reduced(): lax.psum_scatter(part.astype(BF), 'dp', scatter_dimension=0, tiled=True)  58.3 us
    dot_general x3, matrix products, reduced(): part = jnp.einsum('jsrd,jsrf->djf', left, right, preferred_element_type=F32)  32 us
    unnamed x44, local copies, waits for them, and re-layouts  22.4 us
    all_to_all x1, starting transfers between devices, body(): lax.all_to_all(sending.reshape(expert_count, 1, slot_count, model_width),...  14.7 us
  transfers between devices with their start and end apart: 6, of which 4 were waited for; matrix products, arithmetic and copies ran while one was open for 10% of the time, Pallas kernels for 0%

profile of v1, /device:TPU:1, one launch (start us, length us, event | category | flops | bytes accessed | tf_op | source)
XLA Modules:
  0.0 540.2 jit_solution(15996807720750897143)
XLA Ops:
  8.0 0.8 eq.64
  8.9 4.9 convolution_convert_fusion
  13.8 71.2 %all_to_all.41 = bf16[32,1,40,2048]{3,2,1,0:T(8,128)(2,1)S(1)} all-to-all(bf16[32,1,40,2048]{3,2,1,0:T(8,128)(2,1)S(1)} %bitcast.159), channel_id=1, replica_groups=mesh['dp'=8,'expert'=16] {'expert'}, dimensions={0} | all-to-all | bytes 10485760 | tf_op jit(solution)/shard_map/all_to_all | solution.py:24
  85.0 4.4 fusion.5
  89.4 6.5 %multiply_convert_fusion.4 = (bf16[2,16,40,768]{3,2,1,0:T(8,128)(2,1)}, f32[2,16,40,768]{3,2,1,0:T(8,128)}) fusion(f32[2,16,40,768]{3,2,1,0:T(8,128)S(1)} %fusion.5, bf16[2048,2,768,1]{2,1,0,3:T(2,128)(2,1)S(1)} %bitcast.169, bf16[16,2,1,40,2048]{4,3,1,0,2:T(8,128)(2,1)S(1)} %bitcast.161), kind=kOutput, calls=%fused_computation.31 | convolution fusion | flops 4032430080 | bytes 21364736 | tf_op jit(solution)/shard_map/jsrd,djf->jsrf/dot_general | solution.py:34
  96.0 7.7 %fusion.19 = bf16[2,16,40,2048]{3,2,1,0:T(8,128)(2,1)S(1)} fusion(bf16[2,16,40,768]{3,2,1,0:T(8,128)(2,1)} %get-tuple-element.43, bf16[2048,2,768,1]{2,1,0,3:T(2,128)(2,1)} %bitcast.170), kind=kOutput, calls=%fused_computation.28 | convolution fusion | flops 4029153280 | bytes 13500416 | tf_op jit(solution)/shard_map/jsrf,djf->jsrd/dot_general | solution.py:36
  103.6 0.8 fusion.57
  104.4 0.8 fusion.56
  105.2 0.8 fusion.55
  105.9 0.8 fusion.54
  106.7 0.8 fusion.53
  107.4 0.8 fusion.52
  108.2 0.8 fusion.51
  109.0 0.8 fusion.50
  109.7 0.8 fusion.49
  110.5 0.7 fusion.48
  111.2 0.7 fusion.47
  112.0 0.7 fusion.46
  112.7 0.8 fusion.45
  113.5 0.8 fusion.44
  114.2 0.8 fusion.43
  115.0 0.8 fusion.42
  115.8 5.7 %all-to-all-start.1 = ((bf16[16,2,1,40,2048]{4,3,1,2,0:T(8,128)(2,1)}), bf16[16,2,1,40,2048]{4,3,1,2,0:T(8,128)(2,1)}, u32[]{:S(2)}, u32[]{:S(2)}) async-start(bf16[16,2,1,40,2048]{4,3,1,2,0:T(8,128)(2,1)} %fusion.42), calls=%async_computation.1 | async-start | bytes 10485760 | tf_op jit(solution)/shard_map/all_to_all | solution.py:38
  121.5 0.1 eq.68
  121.6 4.3 fusion.38
  125.9 64.9 %all-to-all-done.1 = bf16[16,2,1,40,2048]{4,3,1,2,0:T(8,128)(2,1)} async-done(((bf16[16,2,1,40,2048]{4,3,1,2,0:T(8,128)(2,1)}), bf16[16,2,1,40,2048]{4,3,1,2,0:T(8,128)(2,1)}, u32[]{:S(2)}, u32[]{:S(2)}) %all-to-all-start.1) | async-done | bytes 5242912 | tf_op jit(solution)/shard_map/all_to_all | solution.py:38
  190.8 6.5 %multiply_reduce_fusion.1 = (f32[512]{0:T(512)S(1)}, f32[512,2048]{1,0:T(8,128)S(1)}) fusion(bf16[512,2048]{1,0:T(8,128)(2,1)} %param.12, bf16[1280,2048]{1,0:T(8,128)(2,1)} %bitcast.25, s32[1280]{0:T(1024)S(1)} %eq.64, bf16[1280]{0:T(1024)(128)(2,1)S(1)} %get-tuple-element.42, bf16[512,2048]{1,0:T(8,128)(2,1)S(1)} %copy-done.4), kind=kOutput, calls=%fused_computation.25 | convolution fusion | flops 2691956224 | bytes 13641216 | tf_op jit(solution)/shard_map/dot_general | solution.py:47
  197.3 0.1 select_reduce_fusion.1
  197.4 7.4 %multiply_convert_fusion = (bf16[1280,2048]{1,0:T(8,128)(2,1)}, f32[1280]{0:T(1024)S(1)}) fusion(f32[1280]{0:T(1024)S(1)} %get-tuple-element.41, bf16[16,2,1,40,2048]{4,3,1,2,0:T(8,128)(2,1)} %all-to-all-done.1, f32[512,2048]{1,0:T(8,128)S(1)} %get-tuple-element.46, f32[512]{0:T(512)S(1)} %broadcast_multiply_fusion, s32[1280]{0:T(1024)S(1)} %eq.64), kind=kOutput, calls=%fused_computation.3 | convolution fusion | flops 2700212992 | bytes 14697472 | tf_op jit(solution)/shard_map/dot_general | solution.py:55
  204.8 14.7 %all-to-all-start.2 = ((bf16[32,1,40,2048]{3,2,1,0:T(8,128)(2,1)}), bf16[32,1,40,2048]{3,2,1,0:T(8,128)(2,1)}, u32[]{:S(2)}, u32[]{:S(2)}) async-start(bf16[32,1,40,2048]{3,2,1,0:T(8,128)(2,1)} %bitcast.164), calls=%async_computation.2 | async-start | bytes 10485760 | tf_op jit(solution)/shard_map/all_to_all | solution.py:74
  219.5 0.1 copy.109
  219.7 1.0 convolution_bitcast_fusion
  220.8 0.7 select_maximum_fusion
  221.6 68.4 %all-to-all-done.2 = bf16[32,1,40,2048]{3,2,1,0:T(8,128)(2,1)} async-done(((bf16[32,1,40,2048]{3,2,1,0:T(8,128)(2,1)}), bf16[32,1,40,2048]{3,2,1,0:T(8,128)(2,1)}, u32[]{:S(2)}, u32[]{:S(2)}) %all-to-all-start.2) | async-done | bytes 5242912 | tf_op jit(solution)/shard_map/all_to_all | solution.py:74
  290.0 9.8 %fusion.2 = bf16[2048,2,768]{0,2,1:T(8,128)(2,1)} fusion(bf16[2,16,40,768]{3,2,1,0:T(8,128)(2,1)} %get-tuple-element.43, bf16[16,2,1,40,2048]{4,3,1,0,2:T(8,128)(2,1)} %bitcast.30), kind=kOutput, calls=%fused_computation.8 | convolution fusion | flops 4029677568 | bytes 13500416 | tf_op jit(solution)/shard_map/jsrd,jsrf->djf/dot_general | solution.py:83
  299.9 0.3 reduce-scatter.6.cloned.1.call-start
  300.1 8.2 %fusion.7 = f32[2,16,40,768]{3,2,1,0:T(8,128)S(1)} fusion(bf16[2048,2,768,1]{2,1,0,3:T(2,128)(2,1)} %bitcast.171, bf16[16,2,1,40,2048]{4,3,1,0,2:T(8,128)(2,1)} %bitcast.30), kind=kOutput, calls=%fused_computation.13 | convolution fusion | flops 4026531840 | bytes 15466496 | tf_op jit(solution)/shard_map/jsrd,djf->jsrf/dot_general | solution.py:87
  308.3 1.8 copy-done.10
  310.2 9.9 %fusion.1 = bf16[2048,2,768]{0,2,1:T(8,128)(2,1)} fusion(bf16[16,2,1,40,2048]{4,3,1,0,2:T(8,128)(2,1)} %bitcast.162, f32[2,16,40,768]{3,2,1,0:T(8,128)S(1)} %fusion.7, f32[2,16,40,768]{3,2,1,0:T(8,128)S(1)} %copy-done.9), kind=kOutput, calls=%fused_computation.7 | convolution fusion | flops 4035575808 | bytes 19398656 | tf_op jit(solution)/shard_map/jsrd,jsrf->djf/dot_general | solution.py:83
  320.1 0.0 reduce-scatter.4.cloned.1.call-start
  320.1 12.3 %fusion = bf16[2048,2,768]{0,2,1:T(8,128)(2,1)} fusion(bf16[16,2,1,40,2048]{4,3,1,0,2:T(8,128)(2,1)} %bitcast.163, f32[2,16,40,768]{3,2,1,0:T(8,128)} %copy-done.8, f32[2,16,40,768]{3,2,1,0:T(8,128)} %copy-done.10, f32[2,16,40,768]{3,2,1,0:T(8,128)} %get-tuple-element.44), kind=kOutput, calls=%fused_computation.6 | convolution fusion | flops 4039507968 | bytes 23330816 | tf_op jit(solution)/shard_map/jsrd,jsrf->djf/dot_general | solution.py:83
  332.5 129.6 %all-reduce.3.cloned.1.call-done = f32[2056,32]{0,1:T(8,128)} async-done(((f32[2056,32]{0,1:T(8,128)}), f32[2056,32]{0,1:T(8,128)}) %all-reduce.3.cloned.1.call-update) | async-done | bytes 263184 | tf_op jit(solution)/shard_map/psum | solution.py:73
  462.1 1.7 slice.35
  463.8 1.3 fusion.65
  465.1 3.1 copy.115
  468.2 3.0 copy.114
  471.2 58.3 %reduce-scatter.4.cloned.1.call-done = bf16[256,2,768]{0,2,1:T(8,128)(2,1)} async-done(((bf16[2048,2,768]{0,2,1:T(8,128)(2,1)}), bf16[256,2,768]{0,2,1:T(8,128)(2,1)}) %reduce-scatter.4.cloned.1.call-update) | async-done | bytes 786448 | tf_op jit(solution)/shard_map/reduce_scatter | solution.py:84
  529.5 3.0 copy.113
  (41 shorter events, 0.3 us)
Async XLA Ops:
  8.0 113.6 %copy-start = (bf16[2048,32]{0,1:T(8,128)(2,1)S(1)}, bf16[2048,32]{0,1:T(8,128)(2,1)}, u32[]{:S(2)}) copy-start(bf16[2048,32]{0,1:T(8,128)(2,1)} %param.15) | copy-start | bytes 393220
  13.8 71.2 %copy-start.2 = (bf16[1280,2048]{1,0:T(8,128)(2,1)}, bf16[1280,2048]{1,0:T(8,128)(2,1)S(1)}, u32[]{:S(2)}) copy-start(bf16[1280,2048]{1,0:T(8,128)(2,1)S(1)} %convolution_convert_fusion) | copy-start | bytes 15728644
  13.8 71.2 %copy-start.7 = (bf16[2048,2,768]{2,1,0:T(2,128)(2,1)S(1)}, bf16[2048,2,768]{2,1,0:T(2,128)(2,1)}, u32[]{:S(2)}) copy-start(bf16[2048,2,768]{2,1,0:T(2,128)(2,1)} %param.17) | copy-start | bytes 18874372
  13.8 75.6 %slice-start = ((s8[6291456]{0:T(1024)(128)(4,1)}), s8[4194304]{0:T(1024)(128)(4,1)S(1)}, s32[]{:S(2)}) async-start(s8[6291456]{0:T(1024)(128)(4,1)} %bitcast.167), calls=%async_computation.10 | async-start | bytes 8388608
  85.0 4.4 copy-start.3
  85.0 4.4 slice-start.1
  89.4 6.6 %copy-start.8 = (f32[2,16,40,768]{3,2,1,0:T(8,128)}, f32[2,16,40,768]{3,2,1,0:T(8,128)S(1)}, u32[]{:S(2)}) copy-start(f32[2,16,40,768]{3,2,1,0:T(8,128)S(1)} %fusion.5) | copy-start | bytes 11796484
  115.8 75.0 %all-to-all-start.1 = ((bf16[16,2,1,40,2048]{4,3,1,2,0:T(8,128)(2,1)}), bf16[16,2,1,40,2048]{4,3,1,2,0:T(8,128)(2,1)}, u32[]{:S(2)}, u32[]{:S(2)}) async-start(bf16[16,2,1,40,2048]{4,3,1,2,0:T(8,128)(2,1)} %fusion.42), calls=%async_computation.1 | async-start | bytes 10485760 | tf_op jit(solution)/shard_map/all_to_all | solution.py:38
  121.4 69.3 %copy-start.4 = (bf16[512,2048]{1,0:T(8,128)(2,1)S(1)}, bf16[512,2048]{1,0:T(8,128)(2,1)}, u32[]{:S(2)}) copy-start(bf16[512,2048]{1,0:T(8,128)(2,1)} %param.11) | copy-start | bytes 6291460
  190.8 6.5 %copy-start.5 = (s32[512]{0:T(512)S(1)}, s32[512]{0:T(512)}, u32[]{:S(2)}) copy-start(s32[512]{0:T(512)} %param.13) | copy-start | bytes 6148
  190.8 6.5 %copy-start.6 = (f32[22]{0:T(128)S(1)}, f32[22]{0:T(128)}, u32[]{:S(2)}) copy-start(f32[22]{0:T(128)} %param.14) | copy-start | bytes 268
  204.8 85.2 %all-to-all-start.2 = ((bf16[32,1,40,2048]{3,2,1,0:T(8,128)(2,1)}), bf16[32,1,40,2048]{3,2,1,0:T(8,128)(2,1)}, u32[]{:S(2)}, u32[]{:S(2)}) async-start(bf16[32,1,40,2048]{3,2,1,0:T(8,128)(2,1)} %bitcast.164), calls=%async_computation.2 | async-start | bytes 10485760 | tf_op jit(solution)/shard_map/all_to_all | solution.py:74
  219.5 242.6 %all-reduce.3.cloned.1.call-start = ((), (), s32[]{:S(2)}) async-start(), calls=%async_computation.6 | async-start | bytes 557056 | tf_op jit(solution)/shard_map/psum | solution.py:73
  221.5 243.5 %reduce-scatter.8.cloned.1.call-start = ((), (), s32[]{:S(2)}) async-start(), calls=%async_computation.9 | async-start | bytes 7077888 | tf_op jit(solution)/shard_map/reduce_scatter | solution.py:84
  299.9 168.3 %reduce-scatter.6.cloned.1.call-start = ((), (), s32[]{:S(2)}) async-start(), calls=%async_computation.8 | async-start | bytes 7077888 | tf_op jit(solution)/shard_map/reduce_scatter | solution.py:84
  300.1 10.1 %copy-start.9 = (f32[2,16,40,768]{3,2,1,0:T(8,128)S(1)}, f32[2,16,40,768]{3,2,1,0:T(8,128)}, u32[]{:S(2)}) copy-start(f32[2,16,40,768]{3,2,1,0:T(8,128)} %copy-done.8) | copy-start | bytes 11796484
  308.3 1.9 copy-start.10
  320.1 209.4 %reduce-scatter.4.cloned.1.call-start = ((), (), s32[]{:S(2)}) async-start(), calls=%async_computation.7 | async-start | bytes 7077888 | tf_op jit(solution)/shard_map/reduce_scatter | solution.py:84
  332.4 200.1 %copy-start.1 = (bf16[2048,32]{0,1:T(8,128)(2,1)S(1)}, bf16[2048,32]{0,1:T(8,128)(2,1)}, u32[]{:S(2)}) copy-start(bf16[2048,32]{0,1:T(8,128)(2,1)} %param.15) | copy-start | bytes 393220
Sparse Core Ops, SparseCore 0:
  225.7 236.3 all-reduce.2
Sparse Core Ops, SparseCore 1:
  299.9 81.2 reduce-scatter.7
  383.5 71.8 reduce-scatter.5
  457.6 71.9 reduce-scatter.3
